TPU v7x, 256 devices: a whole 4x4x8 slice. The times are simulated.
256 devices in a mesh: grp: 4 (over z_hi), tile: 64 (over x, z_lo, y, core).
Axes of the slice: x: 4, y: 4, z: 8 (z_hi: 4, z_lo: 2; z = z_hi * 2 + z_lo), core: 2. Of those that a mesh axis runs over, the one named last changes fastest.
Arguments:
- ocean_state: bfloat16 [64, 4096, 512], P(None, 'tile', 'grp'), may hold values from -8 to 8
- sea_mask: int32 [4096, 512], P('tile', 'grp'), may hold values 0 or 1
- spectral_weights: float32 [2, 2, 32, 64, 64], replicated, may hold values from -0.75 to 0.75
- point_weights: bfloat16 [2, 64, 64], replicated, may hold values from -0.75 to 0.75
- point_bias: float32 [2, 64], replicated, may hold values from -4 to 4
- inner_weights: bfloat16 [2, 128, 64], replicated, may hold values from -0.75 to 0.75
- outer_weights: bfloat16 [2, 64, 128], replicated, may hold values from -0.5 to 0.5
- coarse_spectral: float32 [2, 32, 64, 64], replicated, may hold values from -0.75 to 0.75
- coarse_point: float32 [64, 64], replicated, may hold values from -0.75 to 0.75
- coarse_bias: float32 [64], replicated, may hold values from -2.5 to 2.5
Outputs:
- corrected: bfloat16 [64, 4096, 512], P(None, 'tile', 'grp')
Inputs may be any that keep to these rules, and one draw needn't show every extreme that they name: `sea_mask`: 1 marks a sea cell, 0 a land cell.
All inputs are finite; a program needn't handle non-finite values. No bound on the sum of `sea_mask` on one device may be relied on, other than what follows from the above.
Results may differ from a plain program's by a relative error of at most 0.0065.
Values may be sent and summed in bfloat16 or wider, within the bound.
A program may use at most 64 MiB of HBM per device.

v0:
```python
import math
import jax
import jax.numpy as jnp
from jax import lax
from jax.sharding import PartitionSpec as P

H = 64
R = 16
MX = 8
MY = 4
LAYERS = 2
PRECISE = lax.Precision.HIGHEST


def with_halo(x, sides, width):
    for axis, dim in sides:
        devices, length = (lax.axis_size(axis), x.shape[dim])
        up = [(i, (i + 1) % devices) for i in range(devices - 1)]
        down = [(j, i) for i, j in up]
        last = lax.slice_in_dim(x, length - width, length, axis=dim)
        first = lax.slice_in_dim(x, 0, width, axis=dim)
        before = lax.ppermute(last, axis, up)
        after = lax.ppermute(first, axis, down)
        x = jnp.concatenate([before, x, after], axis=dim)
    return x


def wave_numbers():
    order = jnp.arange(MX, dtype=jnp.int32)
    return jnp.where(order < MX // 2, order, order - MX)


def masked_table(positions, numbers, length):
    cycles = positions[:, None] * numbers[None, :] % length
    radians = cycles.astype(jnp.float32) * (2.0 * math.pi / length)
    inside = ((positions >= 0) & (positions < length)).astype(jnp.float32)[:, None]
    return (jnp.cos(radians) * inside, jnp.sin(radians) * inside)


def columns_transform(values, col_positions, col_length):
    channels, row_count, col_count = values.shape
    cos_cols, sin_cols = masked_table(col_positions, jnp.arange(MY, dtype=jnp.int32), col_length)
    lookup = jnp.concatenate([cos_cols, -sin_cols], axis=1)
    flattened = values.reshape(channels * row_count, col_count)
    return jnp.dot(
        flattened, lookup, precision=PRECISE, preferred_element_type=jnp.float32
    ).reshape(channels, row_count, 2 * MY)


def rows_transform(y_modes, row_positions, row_length):
    cos_rows, sin_rows = masked_table(row_positions, wave_numbers(), row_length)
    real_in = y_modes[:, :, :MY]
    imag_in = y_modes[:, :, MY:]
    coef_real = jnp.einsum("cxj,xi->cij", real_in, cos_rows, precision=PRECISE) + jnp.einsum(
        "cxj,xi->cij", imag_in, sin_rows, precision=PRECISE
    )
    coef_imag = jnp.einsum("cxj,xi->cij", imag_in, cos_rows, precision=PRECISE) - jnp.einsum(
        "cxj,xi->cij", real_in, sin_rows, precision=PRECISE
    )
    return jnp.stack([coef_real, coef_imag])


def forward(values, row_positions, col_positions, row_length, col_length):
    return rows_transform(
        columns_transform(values, col_positions, col_length), row_positions, row_length
    )


def mix_modes(coeffs, weights):
    channels = coeffs.shape[1]
    flattened = coeffs.reshape(2, channels, MX * MY)
    weight_real = weights[0]
    weight_imag = weights[1]
    mixed_real = jnp.einsum(
        "koc,ck->ok", weight_real, flattened[0], precision=PRECISE
    ) - jnp.einsum("koc,ck->ok", weight_imag, flattened[1], precision=PRECISE)
    mixed_imag = jnp.einsum(
        "koc,ck->ok", weight_real, flattened[1], precision=PRECISE
    ) + jnp.einsum("koc,ck->ok", weight_imag, flattened[0], precision=PRECISE)
    return (mixed_real, mixed_imag)


def synthesis(mixed_real, mixed_imag, row_positions, col_positions, row_length, col_length):
    channels = mixed_real.shape[0]
    grid_real = mixed_real.reshape(channels, MX, MY)
    grid_imag = mixed_imag.reshape(channels, MX, MY)
    cos_rows, sin_rows = masked_table(row_positions, wave_numbers(), row_length)
    part_real = jnp.einsum("cij,xi->cxj", grid_real, cos_rows, precision=PRECISE) - jnp.einsum(
        "cij,xi->cxj", grid_imag, sin_rows, precision=PRECISE
    )
    part_imag = jnp.einsum("cij,xi->cxj", grid_real, sin_rows, precision=PRECISE) + jnp.einsum(
        "cij,xi->cxj", grid_imag, cos_rows, precision=PRECISE
    )
    cos_cols, sin_cols = masked_table(col_positions, jnp.arange(MY, dtype=jnp.int32), col_length)
    weight = jnp.where(jnp.arange(MY) == 0, 1.0, 2.0).astype(jnp.float32)
    lookup = jnp.concatenate(
        [(cos_cols * weight[None, :]).T, -(sin_cols * weight[None, :]).T], axis=0
    )
    stacked = jnp.concatenate([part_real, part_imag], axis=2)
    row_count = stacked.shape[1]
    result = jnp.dot(stacked.reshape(channels * row_count, 2 * MY), lookup, precision=PRECISE)
    return result.reshape(channels, row_count, col_positions.shape[0])


def finish_layer(
    coeffs, interior, own_mask, ext_rows, ext_cols, spec, w_point, b_point, w_in, w_out
):
    channels, tile_rows, tile_cols = interior.shape
    cell_count = tile_rows * tile_cols
    mixed_real, mixed_imag = mix_modes(coeffs, spec)
    spectral = synthesis(
        mixed_real,
        mixed_imag,
        H + jnp.arange(tile_rows, dtype=jnp.int32),
        H + jnp.arange(tile_cols, dtype=jnp.int32),
        ext_rows,
        ext_cols,
    )
    pre_act = (
        spectral.reshape(channels, cell_count)
        + jnp.dot(
            w_point, interior.reshape(channels, cell_count), preferred_element_type=jnp.float32
        )
        + b_point[:, None]
    )
    activated = jax.nn.gelu(pre_act, approximate=True).astype(jnp.bfloat16)
    hidden = jax.nn.gelu(
        jnp.dot(w_in, activated, preferred_element_type=jnp.float32), approximate=True
    ).astype(jnp.bfloat16)
    result = jnp.dot(w_out, hidden, preferred_element_type=jnp.float32) * own_mask.reshape(
        1, cell_count
    ).astype(jnp.float32)
    return result.reshape(channels, tile_rows, tile_cols).astype(jnp.bfloat16)


def fine_step(interior, own_mask, spec, w_point, b_point, w_in, w_out):
    channels, tile_rows, tile_cols = interior.shape
    ext_rows = tile_rows + 2 * H
    ext_cols = tile_cols + 2 * H
    extended = with_halo(interior, (("grp", 2), ("tile", 1)), H)
    coeffs = forward(
        extended,
        jnp.arange(ext_rows, dtype=jnp.int32),
        jnp.arange(ext_cols, dtype=jnp.int32),
        ext_rows,
        ext_cols,
    )
    coeffs = coeffs / (ext_rows * ext_cols)
    return finish_layer(
        coeffs, interior, own_mask, ext_rows, ext_cols, spec, w_point, b_point, w_in, w_out
    )


def local(
    ocean_state,
    sea_mask,
    spectral_weights,
    point_weights,
    point_bias,
    inner_weights,
    outer_weights,
    coarse_spectral,
    coarse_point,
    coarse_bias,
):
    channels, tile_rows, tile_cols = ocean_state.shape
    current = jnp.where(sea_mask[None] > 0, ocean_state, jnp.zeros((), jnp.bfloat16))
    for layer_index in range(LAYERS):
        current = fine_step(
            current,
            sea_mask,
            spectral_weights[layer_index],
            point_weights[layer_index],
            point_bias[layer_index],
            inner_weights[layer_index],
            outer_weights[layer_index],
        )
    fine_values = current.astype(jnp.float32)
    block_rows = tile_rows // R
    block_cols = tile_cols // R
    coarse = fine_values.reshape(channels, block_rows, R, block_cols, R).sum(axis=(2, 4)) / (R * R)
    grid_rows = block_rows * lax.axis_size("tile")
    grid_cols = block_cols * lax.axis_size("grp")
    row_positions = lax.axis_index("tile") * block_rows + jnp.arange(block_rows, dtype=jnp.int32)
    col_positions = lax.axis_index("grp") * block_cols + jnp.arange(block_cols, dtype=jnp.int32)
    slab_piece = lax.all_gather(coarse, "tile", axis=1, tiled=True)
    piece_rows = slab_piece.shape[1]
    y_modes = columns_transform(slab_piece, col_positions, grid_cols)
    partial_sum = rows_transform(y_modes, jnp.arange(piece_rows, dtype=jnp.int32), grid_rows)
    coeffs = lax.psum(partial_sum, "grp")
    coeffs = coeffs / (grid_rows * grid_cols)
    mixed_real, mixed_imag = mix_modes(coeffs, coarse_spectral)
    spectral = synthesis(mixed_real, mixed_imag, row_positions, col_positions, grid_rows, grid_cols)
    local_term = jnp.dot(
        coarse_point, coarse.reshape(channels, block_rows * block_cols), precision=PRECISE
    )
    correction = (
        spectral + local_term.reshape(channels, block_rows, block_cols) + coarse_bias[:, None, None]
    )
    land_sea = sea_mask.astype(jnp.float32).reshape(1, block_rows, R, block_cols, R)
    corrected = (
        fine_values.reshape(channels, block_rows, R, block_cols, R)
        + correction[:, :, None, :, None] * land_sea
    )
    return corrected.reshape(channels, tile_rows, tile_cols).astype(jnp.bfloat16)


def solution(mesh):
    placed = (P(None, "tile", "grp"), P("tile", "grp"), P(), P(), P(), P(), P(), P(), P(), P())
    return jax.shard_map(
        local, mesh=mesh, in_specs=placed, out_specs=P(None, "tile", "grp"), check_vma=False
    )
```

profile of v0, /device:TPU:64, one launch (start us, length us, event | category | flops | bytes accessed | tf_op | source)
XLA Modules:
  0.0 372.4 jit_solution(2826999524209507329)
XLA Ops:
  0.8 1.3 broadcast_select_fusion
  2.6 6.4 %collective-permute-start = (bf16[64,64,64]{2,1,0:T(8,128)(2,1)S(1)}, bf16[64,64,64]{2,1,0:T(8,128)(2,1)S(1)}, u32[]{:S(2)}, u32[]{:S(2)}) collective-permute-start(bf16[64,64,64]{2,1,0:T(8,128)(2,1)S(1)} %get-tuple-element.7), channel_id=1, source_target_pairs={{0,64},{64,128},{128,192},{1,65},{65,129},{129,193},{2,66},{66,130... | collective-permute-start | bytes 1572872 | tf_op jit(solution)/shard_map/ppermute | solution.py:22
  9.0 1.9 collective-permute-start.1
  10.9 42.9 %collective-permute-done = bf16[64,64,64]{2,1,0:T(8,128)(2,1)S(1)} collective-permute-done((bf16[64,64,64]{2,1,0:T(8,128)(2,1)S(1)}, bf16[64,64,64]{2,1,0:T(8,128)(2,1)S(1)}, u32[]{:S(2)}, u32[]{:S(2)}) %collective-permute-start) | collective-permute-done | bytes 524320 | tf_op jit(solution)/shard_map/ppermute | solution.py:22
  53.8 6.2 %collective-permute-done.1 = bf16[64,64,64]{2,1,0:T(8,128)(2,1)S(1)} collective-permute-done((bf16[64,64,64]{2,1,0:T(8,128)(2,1)S(1)}, bf16[64,64,64]{2,1,0:T(8,128)(2,1)S(1)}, u32[]{:S(2)}, u32[]{:S(2)}) %collective-permute-start.1) | collective-permute-done | bytes 524320 | tf_op jit(solution)/shard_map/ppermute | solution.py:23
  59.9 1.3 pad_maximum_fusion
  61.2 1.6 collective-permute-start.2
  62.8 1.8 collective-permute-start.3
  64.9 1.5 collective-permute-done.2
  66.5 3.9 %collective-permute-done.3 = bf16[64,64,256]{2,1,0:T(8,128)(2,1)S(1)} collective-permute-done((bf16[64,64,256]{2,1,0:T(8,128)(2,1)S(1)}, bf16[64,64,256]{2,1,0:T(8,128)(2,1)S(1)}, u32[]{:S(2)}, u32[]{:S(2)}) %collective-permute-start.3) | collective-permute-done | bytes 2097184 | tf_op jit(solution)/shard_map/ppermute | solution.py:23
  70.4 5.1 %fusion.8 = f32[64,192,8]{1,2,0:T(8,128)S(1)} fusion(bf16[64,64,256]{2,1,0:T(8,128)(2,1)S(1)} %collective-permute-done.3, bf16[64,64,64]{2,1,0:T(8,128)(2,1)S(1)} %collective-permute-done.1, bf16[64,64,128]{2,1,0:T(8,128)(2,1)S(1)} %broadcast_select_fusion, bf16[64,64,64]{2,1,0:T(8,128)(2,1)S(1)} %collective-permute-done, ...), kind=kOutput, calls=%fused_computation.14 | convolution fusion | flops 333449216 | bytes 6692864 | tf_op jit(solution)/shard_map/dot_general | solution.py:45
  77.6 1.7 fusion.92
  79.4 1.7 fusion.98
  81.1 1.7 fusion.96
  82.9 1.7 fusion.94
  86.7 3.6 fusion.273
  90.3 1.6 reshape_reshape.6
  91.9 3.1 fusion.51
  95.0 1.8 fusion.4
  97.6 2.4 collective-permute-start.4
  100.0 4.4 %collective-permute-start.5 = (bf16[64,64,64]{2,1,0:T(8,128)(2,1)S(1)}, bf16[64,64,64]{2,1,0:T(8,128)(2,1)S(1)}, u32[]{:S(2)}, u32[]{:S(2)}) collective-permute-start(bf16[64,64,64]{2,1,0:T(8,128)(2,1)S(1)} %get-tuple-element.6), channel_id=1, source_target_pairs={{64,0},{128,64},{192,128},{65,1},{129,65},{193,129},{66,2},{130,66... | collective-permute-start | bytes 1572872 | tf_op jit(solution)/shard_map/ppermute | solution.py:23
  104.4 10.8 %collective-permute-done.4 = bf16[64,64,64]{2,1,0:T(8,128)(2,1)S(1)} collective-permute-done((bf16[64,64,64]{2,1,0:T(8,128)(2,1)S(1)}, bf16[64,64,64]{2,1,0:T(8,128)(2,1)S(1)}, u32[]{:S(2)}, u32[]{:S(2)}) %collective-permute-start.4) | collective-permute-done | bytes 524320 | tf_op jit(solution)/shard_map/ppermute | solution.py:22
  115.2 3.6 collective-permute-done.5
  118.8 1.3 pad_maximum_fusion.1
  120.1 43.0 %collective-permute-start.6 = (bf16[64,64,256]{2,1,0:T(8,128)(2,1)S(1)}, bf16[64,64,256]{2,1,0:T(8,128)(2,1)}, u32[]{:S(2)}, u32[]{:S(2)}) collective-permute-start(bf16[64,64,256]{2,1,0:T(8,128)(2,1)S(1)} %pad_maximum_fusion.1), channel_id=1, source_target_pairs={{0,1},{1,2},{2,3},{3,4},{4,5},{5,6},{6,7},{7,8},{8,9},{9,10},{10,1... | collective-permute-start | bytes 6291464 | tf_op jit(solution)/shard_map/ppermute | solution.py:22
  163.1 1.5 collective-permute-start.7
  165.7 14.2 %collective-permute-done.7 = bf16[64,64,256]{2,1,0:T(8,128)(2,1)} collective-permute-done((bf16[64,64,256]{2,1,0:T(8,128)(2,1)S(1)}, bf16[64,64,256]{2,1,0:T(8,128)(2,1)}, u32[]{:S(2)}, u32[]{:S(2)}) %collective-permute-start.7) | collective-permute-done | bytes 2097184 | tf_op jit(solution)/shard_map/ppermute | solution.py:23
  179.9 7.6 %fusion.18 = f32[64,192,8]{1,2,0:T(8,128)S(1)} fusion(bf16[64,64,256]{2,1,0:T(8,128)(2,1)} %collective-permute-done.7, bf16[64,64,64]{2,1,0:T(8,128)(2,1)} %copy-done.6, bf16[64,64,128]{2,1,0:T(8,128)(2,1)S(1)} %bitcast.319, bf16[64,64,64]{2,1,0:T(8,128)(2,1)} %copy-done.5, bf16[64,64,256]{2,1,0:T(8,128)(2,1)} %collective-permute-done.6, ...), kind=kOutput, calls=%fused_computation.24 | convolution fusion | flops 333449216 | bytes 6692864 | tf_op jit(solution)/shard_map/dot_general | solution.py:45
  189.7 1.7 fusion.84
  191.4 1.7 fusion.90
  193.2 1.7 fusion.88
  194.9 1.7 fusion.86
  198.8 3.4 fusion.272
  202.2 1.8 reshape_reshape.7
  204.0 3.6 fusion.59
  207.6 3.0 fusion.7
  210.7 2.8 copy.156
  213.4 2.6 reduce_sum.9
  216.1 105.2 %all_gather.3 = f32[64,256,8]{0,2,1:T(8,128)S(1)} all-gather(f32[64,4,8]{0,2,1:T(8,128)S(1)} %broadcast_multiply_fusion.1), channel_id=1, replica_groups=mesh['grp'=4,'tile'=64] {'tile'}, dimensions={1}, use_global_device_ids=true | all-gather | bytes 532480 | tf_op jit(solution)/shard_map/all_gather | solution.py:186
  321.3 7.4 %copy.116 = f32[64,256,8]{2,1,0:T(8,128)} copy(f32[64,256,8]{0,2,1:T(8,128)S(1)} %all_gather.3) | data formatting | bytes 1048576 | tf_op jit(solution)/shard_map/all_gather | solution.py:186
  328.7 9.8 %fusion.201 = f32[64,256,8]{1,2,0:T(8,128)S(1)} fusion(f32[64,256,8]{2,1,0:T(8,128)} %copy.116, f32[8,4]{0,1:T(4,128)S(1)} %get-tuple-element.28, f32[8,4]{0,1:T(4,128)S(1)} %get-tuple-element.27), kind=kOutput, calls=%fused_computation.257 | convolution fusion | flops 12582976 | bytes 1048832 | tf_op jit(solution)/shard_map/dot_general | solution.py:45
  340.6 18.2 %psum.7 = f32[2,64,8,4]{1,2,3,0:T(8,128)S(1)} all-reduce(f32[2,64,8,4]{1,2,3,0:T(8,128)S(1)} %pad_maximum_fusion.4), channel_id=1, replica_groups=mesh['grp'=4,'tile'=64] {'grp'}, use_global_device_ids=true, to_apply=%region_1.2 | all-reduce | flops 4096 | bytes 32768 | tf_op jit(solution)/shard_map/psum | solution.py:190
  358.9 1.7 fusion.80
  360.6 1.7 fusion.78
  362.4 1.7 fusion.76
  364.1 1.7 fusion.82
  368.1 1.5 add_convert_fusion
  369.6 2.3 copy.133
  (110 shorter events, 15.9 us)
Async XLA Ops:
  0.0 367.4 %copy-start = (f32[64,64]{1,0:T(8,128)S(1)}, f32[64,64]{1,0:T(8,128)}, u32[]{:S(2)}) copy-start(f32[64,64]{1,0:T(8,128)} %param.18) | copy-start | bytes 49156
  2.1 62.7 %copy-start.10 = (f32[2,64]{1,0:T(2,128)S(1)}, f32[2,64]{1,0:T(2,128)}, u32[]{:S(2)}) copy-start(f32[2,64]{1,0:T(2,128)} %param.14) | copy-start | bytes 1540
  2.1 62.8 %copy-start.9 = (s32[64,128]{1,0:T(8,128)S(1)}, s32[64,128]{1,0:T(8,128)}, u32[]{:S(2)}) copy-start(s32[64,128]{1,0:T(8,128)} %param.11) | copy-start | bytes 98308
  2.6 51.2 %collective-permute-start = (bf16[64,64,64]{2,1,0:T(8,128)(2,1)S(1)}, bf16[64,64,64]{2,1,0:T(8,128)(2,1)S(1)}, u32[]{:S(2)}, u32[]{:S(2)}) collective-permute-start(bf16[64,64,64]{2,1,0:T(8,128)(2,1)S(1)} %get-tuple-element.7), channel_id=1, source_target_pairs={{0,64},{64,128},{128,192},{1,65},{65,129},{129,193},{2,66},{66,130... | collective-permute-start | bytes 1572872 | tf_op jit(solution)/shard_map/ppermute | solution.py:22
  9.0 51.0 %collective-permute-start.1 = (bf16[64,64,64]{2,1,0:T(8,128)(2,1)S(1)}, bf16[64,64,64]{2,1,0:T(8,128)(2,1)S(1)}, u32[]{:S(2)}, u32[]{:S(2)}) collective-permute-start(bf16[64,64,64]{2,1,0:T(8,128)(2,1)S(1)} %get-tuple-element.8), channel_id=1, source_target_pairs={{64,0},{128,64},{192,128},{65,1},{129,65},{193,129},{66,2},{130,66... | collective-permute-start | bytes 1572872 | tf_op jit(solution)/shard_map/ppermute | solution.py:23
  61.2 5.2 %collective-permute-start.2 = (bf16[64,64,256]{2,1,0:T(8,128)(2,1)S(1)}, bf16[64,64,256]{2,1,0:T(8,128)(2,1)S(1)}, u32[]{:S(2)}, u32[]{:S(2)}) collective-permute-start(bf16[64,64,256]{2,1,0:T(8,128)(2,1)S(1)} %pad_maximum_fusion), channel_id=1, source_target_pairs={{0,1},{1,2},{2,3},{3,4},{4,5},{5,6},{6,7},{7,8},{8,9},{9,10},{10,1... | collective-permute-start | bytes 6291464 | tf_op jit(solution)/shard_map/ppermute | solution.py:22
  62.8 7.6 %collective-permute-start.3 = (bf16[64,64,256]{2,1,0:T(8,128)(2,1)S(1)}, bf16[64,64,256]{2,1,0:T(8,128)(2,1)S(1)}, u32[]{:S(2)}, u32[]{:S(2)}) collective-permute-start(bf16[64,64,256]{2,1,0:T(8,128)(2,1)S(1)} %pad_maximum_fusion), channel_id=1, source_target_pairs={{1,0},{2,1},{3,2},{4,3},{5,4},{6,5},{7,6},{8,7},{9,8},{10,9},{11,1... | collective-permute-start | bytes 6291464 | tf_op jit(solution)/shard_map/ppermute | solution.py:23
  70.4 7.2 %copy-start.2 = (f32[2,2,32,64,64]{4,3,2,1,0:T(8,128)S(1)}, f32[2,2,32,64,64]{4,3,2,1,0:T(8,128)}, u32[]{:S(2)}) copy-start(f32[2,2,32,64,64]{4,3,2,1,0:T(8,128)} %param.12) | copy-start | bytes 6291460
  85.5 6.4 %copy-start.12 = (bf16[2,64,64]{2,1,0:T(8,128)(2,1)S(1)}, bf16[2,64,64]{2,1,0:T(8,128)(2,1)}, u32[]{:S(2)}) copy-start(bf16[2,64,64]{2,1,0:T(8,128)(2,1)} %param.13) | copy-start | bytes 49156
  91.9 3.1 copy-start.13
  91.9 3.1 copy-start.14
  96.8 18.4 %copy-start.7 = (bf16[8192,64]{0,1:T(8,128)(2,1)}, bf16[8192,64]{0,1:T(8,128)(2,1)S(1)}, u32[]{:S(2)}) copy-start(bf16[8192,64]{0,1:T(8,128)(2,1)S(1)} %fusion.4) | copy-start | bytes 3145732
  97.6 17.6 %collective-permute-start.4 = (bf16[64,64,64]{2,1,0:T(8,128)(2,1)S(1)}, bf16[64,64,64]{2,1,0:T(8,128)(2,1)S(1)}, u32[]{:S(2)}, u32[]{:S(2)}) collective-permute-start(bf16[64,64,64]{2,1,0:T(8,128)(2,1)S(1)} %get-tuple-element.5), channel_id=1, source_target_pairs={{0,64},{64,128},{128,192},{1,65},{65,129},{129,193},{2,66},{66,130... | collective-permute-start | bytes 1572872 | tf_op jit(solution)/shard_map/ppermute | solution.py:22
  100.0 18.8 %collective-permute-start.5 = (bf16[64,64,64]{2,1,0:T(8,128)(2,1)S(1)}, bf16[64,64,64]{2,1,0:T(8,128)(2,1)S(1)}, u32[]{:S(2)}, u32[]{:S(2)}) collective-permute-start(bf16[64,64,64]{2,1,0:T(8,128)(2,1)S(1)} %get-tuple-element.6), channel_id=1, source_target_pairs={{64,0},{128,64},{192,128},{65,1},{129,65},{193,129},{66,2},{130,66... | collective-permute-start | bytes 1572872 | tf_op jit(solution)/shard_map/ppermute | solution.py:23
  115.2 49.4 %copy-start.5 = (bf16[64,64,64]{2,1,0:T(8,128)(2,1)}, bf16[64,64,64]{2,1,0:T(8,128)(2,1)S(1)}, u32[]{:S(2)}) copy-start(bf16[64,64,64]{2,1,0:T(8,128)(2,1)S(1)} %collective-permute-done.4) | copy-start | bytes 1572868
  118.8 45.8 %copy-start.6 = (bf16[64,64,64]{2,1,0:T(8,128)(2,1)}, bf16[64,64,64]{2,1,0:T(8,128)(2,1)S(1)}, u32[]{:S(2)}) copy-start(bf16[64,64,64]{2,1,0:T(8,128)(2,1)S(1)} %collective-permute-done.5) | copy-start | bytes 1572868
  120.1 45.6 %collective-permute-start.6 = (bf16[64,64,256]{2,1,0:T(8,128)(2,1)S(1)}, bf16[64,64,256]{2,1,0:T(8,128)(2,1)}, u32[]{:S(2)}, u32[]{:S(2)}) collective-permute-start(bf16[64,64,256]{2,1,0:T(8,128)(2,1)S(1)} %pad_maximum_fusion.1), channel_id=1, source_target_pairs={{0,1},{1,2},{2,3},{3,4},{4,5},{5,6},{6,7},{7,8},{8,9},{9,10},{10,1... | collective-permute-start | bytes 6291464 | tf_op jit(solution)/shard_map/ppermute | solution.py:22
  163.1 16.8 %collective-permute-start.7 = (bf16[64,64,256]{2,1,0:T(8,128)(2,1)S(1)}, bf16[64,64,256]{2,1,0:T(8,128)(2,1)}, u32[]{:S(2)}, u32[]{:S(2)}) collective-permute-start(bf16[64,64,256]{2,1,0:T(8,128)(2,1)S(1)} %pad_maximum_fusion.1), channel_id=1, source_target_pairs={{1,0},{2,1},{3,2},{4,3},{5,4},{6,5},{7,6},{8,7},{9,8},{10,9},{11,1... | collective-permute-start | bytes 6291464 | tf_op jit(solution)/shard_map/ppermute | solution.py:23
  164.8 24.8 %copy-start.3 = (f32[2,2,32,64,64]{4,3,2,1,0:T(8,128)S(1)}, f32[2,2,32,64,64]{4,3,2,1,0:T(8,128)}, u32[]{:S(2)}) copy-start(f32[2,2,32,64,64]{4,3,2,1,0:T(8,128)} %param.12) | copy-start | bytes 6291460
  197.6 6.4 %copy-start.8 = (bf16[8192,64]{0,1:T(8,128)(2,1)S(1)}, bf16[8192,64]{0,1:T(8,128)(2,1)}, u32[]{:S(2)}) copy-start(bf16[8192,64]{0,1:T(8,128)(2,1)} %copy-done.7) | copy-start | bytes 3145732
  328.7 30.2 %copy-start.4 = (f32[2,32,64,64]{3,2,1,0:T(8,128)S(1)}, f32[2,32,64,64]{3,2,1,0:T(8,128)}, u32[]{:S(2)}) copy-start(f32[2,32,64,64]{3,2,1,0:T(8,128)} %param.17) | copy-start | bytes 3145732
  338.5 28.9 %copy-start.11 = (f32[64]{0:T(128)S(1)}, f32[64]{0:T(128)}, u32[]{:S(2)}) copy-start(f32[64]{0:T(128)} %param.19) | copy-start | bytes 772
  360.6 7.5 %copy-start.1 = (f32[64,8192]{0,1:T(8,128)S(1)}, f32[64,8192]{0,1:T(8,128)}, u32[]{:S(2)}) copy-start(f32[64,8192]{0,1:T(8,128)} %copy.156) | copy-start | bytes 6291460
where the time goes:
time: 376 us; the launch traced here: 372 us
  blocking collectives  123 us (33%)
  waiting for transfers between devices  84 us (22%)
  matrix products  73.1 us (19%)
  starting transfers between devices  63 us (17%)
  local copies, waits for them, and re-layouts  18.4 us (5%)
  other arithmetic  9.35 us (2%)
    all_gather x1, blocking collectives, local(): slab_piece = lax.all_gather(coarse, 'tile', axis=1, tiled=True)  105 us
    ppermute x4, waiting for transfers between devices, with_halo(): before = lax.ppermute(last, axis, up)  56 us
    ppermute x4, starting transfers between devices, with_halo(): before = lax.ppermute(last, axis, up)  53.4 us
    ppermute x4, waiting for transfers between devices, with_halo(): after = lax.ppermute(first, axis, down)  28 us
    dot_general x3, matrix products, columns_transform(): jnp.dot(flattened, lookup, precision=PRECISE, preferred_element_type=jnp....  22.5 us
    psum x1, blocking collectives, local(): coeffs = lax.psum(partial_sum, 'grp')  18.2 us
    ppermute x4, starting transfers between devices, with_halo(): after = lax.ppermute(first, axis, down)  9.62 us
  transfers between devices with their start and end apart: 8, of which 8 were waited for; matrix products, arithmetic and copies ran while one was open for 0% of the time, Pallas kernels for 0%

commit v1 on v0

--- a/solution.py
+++ b/solution.py
@@ -3,6 +3,7 @@
 import jax.numpy as jnp
 from jax import lax
 from jax.sharding import PartitionSpec as P
+from jax.lax import all_to_all, axis_size
 
 H = 64
 R = 16
@@ -10,6 +11,12 @@
 MY = 4
 LAYERS = 2
 PRECISE = lax.Precision.HIGHEST
+move_the_boxes = lambda page, mesh_name, array_dim: jnp.concatenate(
+    all_to_all(
+        jnp.stack(axis_size(mesh_name) * [page]), axis_name=mesh_name, split_axis=0, concat_axis=0
+    ),
+    axis=array_dim,
+)
 
 
 def with_halo(x, sides, width):
@@ -183,7 +190,7 @@
     grid_cols = block_cols * lax.axis_size("grp")
     row_positions = lax.axis_index("tile") * block_rows + jnp.arange(block_rows, dtype=jnp.int32)
     col_positions = lax.axis_index("grp") * block_cols + jnp.arange(block_cols, dtype=jnp.int32)
-    slab_piece = lax.all_gather(coarse, "tile", axis=1, tiled=True)
+    slab_piece = move_the_boxes(coarse, "tile", 1)
     piece_rows = slab_piece.shape[1]
     y_modes = columns_transform(slab_piece, col_positions, grid_cols)
     partial_sum = rows_transform(y_modes, jnp.arange(piece_rows, dtype=jnp.int32), grid_rows)

time: 376 us -> 307 us (0.82)
  blocking collectives: 123 us -> 17.9 us
  starting transfers between devices: 63 us -> 95.8 us
  waiting for transfers between devices: 84 us -> 97.5 us
  matrix products: 73.1 us -> 62.7 us
    all_gather x1 -> x0, blocking collectives: 105 us -> none  [local(): slab_piece = lax.all_gather(coarse, 'tile', axis=1, tiled=True)]
    all_to_all x0 -> x1, starting transfers between devices: none -> 33.8 us  [all_to_all(jnp.stack(axis_size(mesh_name) * [page]), axis_name=mesh_name,...]
    all_to_all x0 -> x1, waiting for transfers between devices: none -> 12.2 us  [all_to_all(jnp.stack(axis_size(mesh_name) * [page]), axis_name=mesh_name,...]
    dot_general x3, matrix products: 22.5 us -> 11.7 us  [columns_transform(): jnp.dot(flattened, lookup, precision=PRECISE, preferred_element_type=jnp....]
    all_gather x1 -> x0, local copies, waits for them, and re-layouts: 7.39 us -> none  [local(): slab_piece = lax.all_gather(coarse, 'tile', axis=1, tiled=True)]
  transfers between devices with their start and end apart: 8 -> 9, of which waited for: 8 -> 9; matrix products, arithmetic and copies ran while one was open for 0% -> 0% of each run, Pallas kernels for 0% -> 0%
where the time goes in v1:
time: 307 us; the launch traced here: 302 us
  waiting for transfers between devices  97.5 us (32%)
  starting transfers between devices  95.8 us (31%)
  matrix products  62.7 us (20%)
  blocking collectives  17.9 us (6%)
  local copies, waits for them, and re-layouts  15.5 us (5%)
  other arithmetic  12.1 us (4%)
    ppermute x4, waiting for transfers between devices, with_halo(): before = lax.ppermute(last, axis, up)  57.3 us
    ppermute x4, starting transfers between devices, with_halo(): before = lax.ppermute(last, axis, up)  52.4 us
    all_to_all x1, starting transfers between devices, all_to_all(jnp.stack(axis_size(mesh_name) * [page]), axis_name=mesh_name,...  33.8 us
    ppermute x4, waiting for transfers between devices, with_halo(): after = lax.ppermute(first, axis, down)  28 us
    psum x1, blocking collectives, local(): coeffs = lax.psum(partial_sum, 'grp')  17.9 us
    all_to_all x1, waiting for transfers between devices, all_to_all(jnp.stack(axis_size(mesh_name) * [page]), axis_name=mesh_name,...  12.2 us
    dot_general x3, matrix products, columns_transform(): jnp.dot(flattened, lookup, precision=PRECISE, preferred_element_type=jnp....  11.7 us
    ppermute x4, starting transfers between devices, with_halo(): after = lax.ppermute(first, axis, down)  9.64 us
  transfers between devices with their start and end apart: 9, of which 9 were waited for; matrix products, arithmetic and copies ran while one was open for 0% of the time, Pallas kernels for 0%

profile of v1, /device:TPU:64, one launch (start us, length us, event | category | flops | bytes accessed | tf_op | source)
XLA Modules:
  0.0 302.4 jit_solution(5410705029497908210)
XLA Ops:
  2.6 6.4 %collective-permute-start = (bf16[64,64,64]{2,1,0:T(8,128)(2,1)S(1)}, bf16[64,64,64]{2,1,0:T(8,128)(2,1)S(1)}, u32[]{:S(2)}, u32[]{:S(2)}) collective-permute-start(bf16[64,64,64]{2,1,0:T(8,128)(2,1)S(1)} %get-tuple-element.7), channel_id=1, source_target_pairs={{0,64},{64,128},{128,192},{1,65},{65,129},{129,193},{2,66},{66,130... | collective-permute-start | bytes 1572872 | tf_op jit(solution)/shard_map/ppermute | solution.py:29
  9.0 1.9 collective-permute-start.1
  10.9 42.9 %collective-permute-done = bf16[64,64,64]{2,1,0:T(8,128)(2,1)S(1)} collective-permute-done((bf16[64,64,64]{2,1,0:T(8,128)(2,1)S(1)}, bf16[64,64,64]{2,1,0:T(8,128)(2,1)S(1)}, u32[]{:S(2)}, u32[]{:S(2)}) %collective-permute-start) | collective-permute-done | bytes 524320 | tf_op jit(solution)/shard_map/ppermute | solution.py:29
  53.8 6.2 %collective-permute-done.1 = bf16[64,64,64]{2,1,0:T(8,128)(2,1)S(1)} collective-permute-done((bf16[64,64,64]{2,1,0:T(8,128)(2,1)S(1)}, bf16[64,64,64]{2,1,0:T(8,128)(2,1)S(1)}, u32[]{:S(2)}, u32[]{:S(2)}) %collective-permute-start.1) | collective-permute-done | bytes 524320 | tf_op jit(solution)/shard_map/ppermute | solution.py:30
  61.2 1.6 collective-permute-start.2
  62.8 1.8 collective-permute-start.3
  64.9 1.5 collective-permute-done.2
  66.5 3.9 %collective-permute-done.3 = bf16[64,64,256]{2,1,0:T(8,128)(2,1)S(1)} collective-permute-done((bf16[64,64,256]{2,1,0:T(8,128)(2,1)S(1)}, bf16[64,64,256]{2,1,0:T(8,128)(2,1)S(1)}, u32[]{:S(2)}, u32[]{:S(2)}) %collective-permute-start.3) | collective-permute-done | bytes 2097184 | tf_op jit(solution)/shard_map/ppermute | solution.py:30
  70.4 5.1 %fusion.8 = f32[64,192,8]{1,2,0:T(8,128)S(1)} fusion(bf16[64,64,256]{2,1,0:T(8,128)(2,1)S(1)} %collective-permute-done.3, bf16[64,64,64]{2,1,0:T(8,128)(2,1)S(1)} %collective-permute-done.1, bf16[64,64,128]{2,1,0:T(8,128)(2,1)S(1)} %broadcast_select_fusion, bf16[64,64,64]{2,1,0:T(8,128)(2,1)S(1)} %collective-permute-done, ...), kind=kOutput, calls=%fused_computation.14 | convolution fusion | flops 333449216 | bytes 6692864 | tf_op jit(solution)/shard_map/dot_general | solution.py:52
  77.6 1.7 fusion.90
  79.4 1.7 fusion.96
  81.1 1.7 fusion.94
  82.9 1.7 fusion.92
  86.7 3.6 %fusion.277 = f32[4096,128]{1,0:T(8,128)S(1)} fusion(f32[4096,8]{0,1:T(8,128)S(1)} %reshape.178, f32[4,128]{1,0:T(4,128)S(1)} %get-tuple-element.26, f32[4,128]{1,0:T(4,128)S(1)} %get-tuple-element.25), kind=kOutput, calls=%fused_computation.330 | convolution fusion | flops 50332672 | bytes 2232320 | tf_op jit(solution)/shard_map/dot_general | solution.py:108
  90.3 1.5 reshape_reshape.7
  91.9 3.1 %fusion.51 = bf16[64,8192]{1,0:T(8,128)(2,1)S(1)} fusion(f32[64,8192]{1,0:T(8,128)} %reshape_reshape.7, bf16[8,8,64,128]{3,2,1,0:T(8,128)(2,1)S(1)} %bitcast.320, f32[64]{0:T(128)S(1)} %get-tuple-element.30, bf16[2,64,64]{2,1,0:T(8,128)(2,1)S(1)} %copy-done.8), kind=kOutput, calls=%fused_computation.62 | convolution fusion | flops 72876032 | bytes 4211200 | tf_op jit(solution)/shard_map/dot_general | solution.py:128
  95.0 1.8 fusion.4
  97.5 2.4 collective-permute-start.4
  100.0 4.4 %collective-permute-start.5 = (bf16[64,64,64]{2,1,0:T(8,128)(2,1)S(1)}, bf16[64,64,64]{2,1,0:T(8,128)(2,1)S(1)}, u32[]{:S(2)}, u32[]{:S(2)}) collective-permute-start(bf16[64,64,64]{2,1,0:T(8,128)(2,1)S(1)} %get-tuple-element.6), channel_id=1, source_target_pairs={{64,0},{128,64},{192,128},{65,1},{129,65},{193,129},{66,2},{130,66... | collective-permute-start | bytes 1572872 | tf_op jit(solution)/shard_map/ppermute | solution.py:30
  104.4 10.8 %collective-permute-done.4 = bf16[64,64,64]{2,1,0:T(8,128)(2,1)S(1)} collective-permute-done((bf16[64,64,64]{2,1,0:T(8,128)(2,1)S(1)}, bf16[64,64,64]{2,1,0:T(8,128)(2,1)S(1)}, u32[]{:S(2)}, u32[]{:S(2)}) %collective-permute-start.4) | collective-permute-done | bytes 524320 | tf_op jit(solution)/shard_map/ppermute | solution.py:29
  115.1 3.6 %collective-permute-done.5 = bf16[64,64,64]{2,1,0:T(8,128)(2,1)S(1)} collective-permute-done((bf16[64,64,64]{2,1,0:T(8,128)(2,1)S(1)}, bf16[64,64,64]{2,1,0:T(8,128)(2,1)S(1)}, u32[]{:S(2)}, u32[]{:S(2)}) %collective-permute-start.5) | collective-permute-done | bytes 524320 | tf_op jit(solution)/shard_map/ppermute | solution.py:30
  120.1 42.0 %collective-permute-start.6 = (bf16[64,64,256]{2,1,0:T(8,128)(2,1)S(1)}, bf16[64,64,256]{2,1,0:T(8,128)(2,1)S(1)}, u32[]{:S(2)}, u32[]{:S(2)}) collective-permute-start(bf16[64,64,256]{2,1,0:T(8,128)(2,1)S(1)} %pad_maximum_fusion.1), channel_id=1, source_target_pairs={{0,1},{1,2},{2,3},{3,4},{4,5},{5,6},{6,7},{7,8},{8,9},{9,10},{10,1... | collective-permute-start | bytes 6291464 | tf_op jit(solution)/shard_map/ppermute | solution.py:29
  162.1 1.5 collective-permute-start.7
  163.6 2.1 collective-permute-done.6
  165.7 14.2 %collective-permute-done.7 = bf16[64,64,256]{2,1,0:T(8,128)(2,1)S(1)} collective-permute-done((bf16[64,64,256]{2,1,0:T(8,128)(2,1)S(1)}, bf16[64,64,256]{2,1,0:T(8,128)(2,1)S(1)}, u32[]{:S(2)}, u32[]{:S(2)}) %collective-permute-start.7) | collective-permute-done | bytes 2097184 | tf_op jit(solution)/shard_map/ppermute | solution.py:30
  180.0 5.0 %fusion.18 = f32[64,192,8]{1,2,0:T(8,128)S(1)} fusion(bf16[64,64,256]{2,1,0:T(8,128)(2,1)S(1)} %collective-permute-done.7, bf16[64,64,64]{2,1,0:T(8,128)(2,1)S(1)} %collective-permute-done.5, bf16[64,64,128]{2,1,0:T(8,128)(2,1)S(1)} %bitcast.323, bf16[64,64,64]{2,1,0:T(8,128)(2,1)S(1)} %collective-permute-done.4, ...), kind=kOutput, calls=%fused_computation.24 | convolution fusion | flops 333449216 | bytes 6692864 | tf_op jit(solution)/shard_map/dot_general | solution.py:52
  187.2 1.7 fusion.82
  188.9 1.7 fusion.88
  190.7 1.7 fusion.86
  192.4 1.7 fusion.84
  196.3 3.8 %fusion.276 = f32[4096,128]{1,0:T(8,128)S(1)} fusion(f32[4096,8]{0,1:T(8,128)S(1)} %reshape.182, f32[4,128]{1,0:T(4,128)S(1)} %get-tuple-element.26, f32[4,128]{1,0:T(4,128)S(1)} %get-tuple-element.25), kind=kOutput, calls=%fused_computation.329 | convolution fusion | flops 50332672 | bytes 2232320 | tf_op jit(solution)/shard_map/dot_general | solution.py:108
  200.1 1.5 reshape_reshape.8
  201.6 3.6 %fusion.59 = bf16[64,8192]{1,0:T(8,128)(2,1)} fusion(f32[64,8192]{1,0:T(8,128)} %reshape_reshape.8, bf16[8192,64]{0,1:T(8,128)(2,1)S(1)} %fusion.4, f32[64]{0:T(128)S(1)} %get-tuple-element.29, bf16[2,64,64]{2,1,0:T(8,128)(2,1)S(1)} %copy-done.8), kind=kOutput, calls=%fused_computation.70 | convolution fusion | flops 72876032 | bytes 4211200 | tf_op jit(solution)/shard_map/dot_general | solution.py:128
  205.2 3.0 %fusion.7 = f32[64,8192]{1,0:T(8,128)S(1)} fusion(bf16[64,8192]{1,0:T(8,128)(2,1)} %fusion.59, f32[8192]{0:T(1024)S(1)} %get-tuple-element.16, bf16[2,64,128]{2,1,0:T(8,128)(2,1)S(1)} %copy-done.9, bf16[2,128,64]{1,2,0:T(8,128)(2,1)S(1)} %copy-done.10), kind=kOutput, calls=%fused_computation.13 | convolution fusion | flops 279445504 | bytes 3211264 | tf_op jit(solution)/shard_map/dot_general | solution.py:137
  208.3 2.7 copy.80
  211.0 2.6 reduce_sum.9
  213.8 1.5 reshape.218
  215.2 33.8 %all-to-all-start = ((f32[64,1,2048]{2,1,0:T(1,128)}), f32[64,1,2048]{2,1,0:T(1,128)S(1)}, u32[]{:S(2)}, u32[]{:S(2)}) async-start(f32[64,1,2048]{2,1,0:T(1,128)} %reshape.218), calls=%async_computation | async-start | bytes 1048576 | tf_op jit(solution)/shard_map/all_to_all | solution.py:15
  249.2 12.2 %all-to-all-done = f32[64,1,2048]{2,1,0:T(1,128)S(1)} async-done(((f32[64,1,2048]{2,1,0:T(1,128)}), f32[64,1,2048]{2,1,0:T(1,128)S(1)}, u32[]{:S(2)}, u32[]{:S(2)}) %all-to-all-start) | async-done | bytes 524320 | tf_op jit(solution)/shard_map/all_to_all | solution.py:15
  262.0 2.8 reduce
  267.4 1.6 fusion.205
  271.2 17.9 %psum.7 = f32[2,64,8,4]{1,2,3,0:T(8,128)S(1)} all-reduce(f32[2,64,8,4]{1,2,3,0:T(8,128)S(1)} %pad_maximum_fusion.4), channel_id=1, replica_groups=mesh['grp'=4,'tile'=64] {'grp'}, use_global_device_ids=true, to_apply=%region_1.2 | all-reduce | flops 4096 | bytes 32768 | tf_op jit(solution)/shard_map/psum | solution.py:197
  289.1 1.7 fusion.80
  290.9 1.7 fusion.76
  293.3 1.8 fusion.78
  295.0 1.7 fusion.74
  298.3 1.5 add_convert_fusion
  299.8 2.3 copy.55
  (108 shorter events, 22.3 us)
Async XLA Ops:
  0.0 297.6 %copy-start = (f32[64,64]{1,0:T(8,128)S(1)}, f32[64,64]{1,0:T(8,128)}, u32[]{:S(2)}) copy-start(f32[64,64]{1,0:T(8,128)} %param.18) | copy-start | bytes 49156
  2.1 62.7 %copy-start.6 = (f32[2,64]{1,0:T(2,128)S(1)}, f32[2,64]{1,0:T(2,128)}, u32[]{:S(2)}) copy-start(f32[2,64]{1,0:T(2,128)} %param.14) | copy-start | bytes 1540
  2.1 62.8 %copy-start.5 = (s32[64,128]{1,0:T(8,128)S(1)}, s32[64,128]{1,0:T(8,128)}, u32[]{:S(2)}) copy-start(s32[64,128]{1,0:T(8,128)} %param.11) | copy-start | bytes 98308
  2.6 51.2 %collective-permute-start = (bf16[64,64,64]{2,1,0:T(8,128)(2,1)S(1)}, bf16[64,64,64]{2,1,0:T(8,128)(2,1)S(1)}, u32[]{:S(2)}, u32[]{:S(2)}) collective-permute-start(bf16[64,64,64]{2,1,0:T(8,128)(2,1)S(1)} %get-tuple-element.7), channel_id=1, source_target_pairs={{0,64},{64,128},{128,192},{1,65},{65,129},{129,193},{2,66},{66,130... | collective-permute-start | bytes 1572872 | tf_op jit(solution)/shard_map/ppermute | solution.py:29
  9.0 51.0 %collective-permute-start.1 = (bf16[64,64,64]{2,1,0:T(8,128)(2,1)S(1)}, bf16[64,64,64]{2,1,0:T(8,128)(2,1)S(1)}, u32[]{:S(2)}, u32[]{:S(2)}) collective-permute-start(bf16[64,64,64]{2,1,0:T(8,128)(2,1)S(1)} %get-tuple-element.8), channel_id=1, source_target_pairs={{64,0},{128,64},{192,128},{65,1},{129,65},{193,129},{66,2},{130,66... | collective-permute-start | bytes 1572872 | tf_op jit(solution)/shard_map/ppermute | solution.py:30
  61.2 5.2 %collective-permute-start.2 = (bf16[64,64,256]{2,1,0:T(8,128)(2,1)S(1)}, bf16[64,64,256]{2,1,0:T(8,128)(2,1)S(1)}, u32[]{:S(2)}, u32[]{:S(2)}) collective-permute-start(bf16[64,64,256]{2,1,0:T(8,128)(2,1)S(1)} %pad_maximum_fusion), channel_id=1, source_target_pairs={{0,1},{1,2},{2,3},{3,4},{4,5},{5,6},{6,7},{7,8},{8,9},{9,10},{10,1... | collective-permute-start | bytes 6291464 | tf_op jit(solution)/shard_map/ppermute | solution.py:29
  62.8 7.6 %collective-permute-start.3 = (bf16[64,64,256]{2,1,0:T(8,128)(2,1)S(1)}, bf16[64,64,256]{2,1,0:T(8,128)(2,1)S(1)}, u32[]{:S(2)}, u32[]{:S(2)}) collective-permute-start(bf16[64,64,256]{2,1,0:T(8,128)(2,1)S(1)} %pad_maximum_fusion), channel_id=1, source_target_pairs={{1,0},{2,1},{3,2},{4,3},{5,4},{6,5},{7,6},{8,7},{9,8},{10,9},{11,1... | collective-permute-start | bytes 6291464 | tf_op jit(solution)/shard_map/ppermute | solution.py:30
  70.4 7.2 %copy-start.2 = (f32[2,2,32,64,64]{4,3,2,1,0:T(8,128)S(1)}, f32[2,2,32,64,64]{4,3,2,1,0:T(8,128)}, u32[]{:S(2)}) copy-start(f32[2,2,32,64,64]{4,3,2,1,0:T(8,128)} %param.12) | copy-start | bytes 6291460
  85.5 6.3 %copy-start.8 = (bf16[2,64,64]{2,1,0:T(8,128)(2,1)S(1)}, bf16[2,64,64]{2,1,0:T(8,128)(2,1)}, u32[]{:S(2)}) copy-start(bf16[2,64,64]{2,1,0:T(8,128)(2,1)} %param.13) | copy-start | bytes 49156
  91.9 3.1 %copy-start.9 = (bf16[2,64,128]{2,1,0:T(8,128)(2,1)S(1)}, bf16[2,64,128]{2,1,0:T(8,128)(2,1)}, u32[]{:S(2)}) copy-start(bf16[2,64,128]{2,1,0:T(8,128)(2,1)} %param.16) | copy-start | bytes 98308
  91.9 3.1 %copy-start.10 = (bf16[2,128,64]{1,2,0:T(8,128)(2,1)S(1)}, bf16[2,128,64]{1,2,0:T(8,128)(2,1)}, u32[]{:S(2)}) copy-start(bf16[2,128,64]{1,2,0:T(8,128)(2,1)} %param.15) | copy-start | bytes 98308
  97.5 17.6 %collective-permute-start.4 = (bf16[64,64,64]{2,1,0:T(8,128)(2,1)S(1)}, bf16[64,64,64]{2,1,0:T(8,128)(2,1)S(1)}, u32[]{:S(2)}, u32[]{:S(2)}) collective-permute-start(bf16[64,64,64]{2,1,0:T(8,128)(2,1)S(1)} %get-tuple-element.5), channel_id=1, source_target_pairs={{0,64},{64,128},{128,192},{1,65},{65,129},{129,193},{2,66},{66,130... | collective-permute-start | bytes 1572872 | tf_op jit(solution)/shard_map/ppermute | solution.py:29
  100.0 18.8 %collective-permute-start.5 = (bf16[64,64,64]{2,1,0:T(8,128)(2,1)S(1)}, bf16[64,64,64]{2,1,0:T(8,128)(2,1)S(1)}, u32[]{:S(2)}, u32[]{:S(2)}) collective-permute-start(bf16[64,64,64]{2,1,0:T(8,128)(2,1)S(1)} %get-tuple-element.6), channel_id=1, source_target_pairs={{64,0},{128,64},{192,128},{65,1},{129,65},{193,129},{66,2},{130,66... | collective-permute-start | bytes 1572872 | tf_op jit(solution)/shard_map/ppermute | solution.py:30
  120.0 67.1 %copy-start.3 = (f32[2,2,32,64,64]{4,3,2,1,0:T(8,128)S(1)}, f32[2,2,32,64,64]{4,3,2,1,0:T(8,128)}, u32[]{:S(2)}) copy-start(f32[2,2,32,64,64]{4,3,2,1,0:T(8,128)} %param.12) | copy-start | bytes 6291460
  120.1 45.7 %collective-permute-start.6 = (bf16[64,64,256]{2,1,0:T(8,128)(2,1)S(1)}, bf16[64,64,256]{2,1,0:T(8,128)(2,1)S(1)}, u32[]{:S(2)}, u32[]{:S(2)}) collective-permute-start(bf16[64,64,256]{2,1,0:T(8,128)(2,1)S(1)} %pad_maximum_fusion.1), channel_id=1, source_target_pairs={{0,1},{1,2},{2,3},{3,4},{4,5},{5,6},{6,7},{7,8},{8,9},{9,10},{10,1... | collective-permute-start | bytes 6291464 | tf_op jit(solution)/shard_map/ppermute | solution.py:29
  162.1 17.9 %collective-permute-start.7 = (bf16[64,64,256]{2,1,0:T(8,128)(2,1)S(1)}, bf16[64,64,256]{2,1,0:T(8,128)(2,1)S(1)}, u32[]{:S(2)}, u32[]{:S(2)}) collective-permute-start(bf16[64,64,256]{2,1,0:T(8,128)(2,1)S(1)} %pad_maximum_fusion.1), channel_id=1, source_target_pairs={{1,0},{2,1},{3,2},{4,3},{5,4},{6,5},{7,6},{8,7},{9,8},{10,9},{11,1... | collective-permute-start | bytes 6291464 | tf_op jit(solution)/shard_map/ppermute | solution.py:30
  215.2 73.9 %copy-start.4 = (f32[2,32,64,64]{3,2,1,0:T(8,128)S(1)}, f32[2,32,64,64]{3,2,1,0:T(8,128)}, u32[]{:S(2)}) copy-start(f32[2,32,64,64]{3,2,1,0:T(8,128)} %param.17) | copy-start | bytes 3145732
  215.2 46.2 %all-to-all-start = ((f32[64,1,2048]{2,1,0:T(1,128)}), f32[64,1,2048]{2,1,0:T(1,128)S(1)}, u32[]{:S(2)}, u32[]{:S(2)}) async-start(f32[64,1,2048]{2,1,0:T(1,128)} %reshape.218), calls=%async_computation | async-start | bytes 1048576 | tf_op jit(solution)/shard_map/all_to_all | solution.py:15
  267.4 30.2 %copy-start.7 = (f32[64]{0:T(128)S(1)}, f32[64]{0:T(128)}, u32[]{:S(2)}) copy-start(f32[64]{0:T(128)} %param.19) | copy-start | bytes 772
  290.9 7.5 %copy-start.1 = (f32[64,8192]{0,1:T(8,128)S(1)}, f32[64,8192]{0,1:T(8,128)}, u32[]{:S(2)}) copy-start(f32[64,8192]{0,1:T(8,128)} %copy.80) | copy-start | bytes 6291460
